TPU v7x, 512 devices: a whole 4x4x16 slice. The times are simulated.
512 devices in a mesh: req: 64 (over z_lo, x, core), tp: 8 (over y, z_hi).
Axes of the slice: x: 4, y: 4, z: 16 (z_hi: 2, z_lo: 8; z = z_hi * 8 + z_lo), core: 2. Of those that a mesh axis runs over, the one named last changes fastest.
Arguments:
- block_x: bfloat16 [24576, 4096], P('req', 'tp'), may hold values from -400 to 400
- decode_x: bfloat16 [2048, 4096], P('req', 'tp'), may hold values from -400 to 400
- gain: bfloat16 [4096], replicated, may hold values from 0.099609375 to 1.8984375
- w_qkv: bfloat16 [4096, 6144], P(None, 'tp'), may hold values from -0.09375 to 0.09375
- ctx_cache: bfloat16 [65536, 2048], P('req', 'tp'), may hold values from -500 to 500
- prompt_cache: bfloat16 [32768, 2048], P('req', 'tp'), may hold values from -500 to 500
- tail_pool: bfloat16 [131072, 2048], P('req', 'tp'), may hold values from -500 to 500
- page_table: int32 [64, 128], P('req'), may hold values from 0 to 127, each once within a row
- tail_len: int32 [64, 32], P('req'), may hold values from 1 to 64, 1280 in all within a row
- block_offset: int32 [64], P('req'), may hold values from 256 to 1024, as said below
- move_mask: int32 [1], replicated, may hold values from 1 to 63
Outputs:
- block_out: bfloat16 [24576, 4096], P('req', 'tp')
- decode_out: bfloat16 [2048, 4096], P('req', 'tp')
Inputs may be any that keep to these rules, and one draw needn't show every extreme that they name: `page_table`: each row is a permutation of 0 to 127. `tail_len`: each row sums to 1280 and holds 64 at least once. `block_offset`: some request has exactly 1024 in every draw.
All inputs are finite; a program needn't handle non-finite values.
Results may differ from a plain program's by a relative error of at most 0.0065.
The roundings to bfloat16 on the way count: a program that leaves them out, or rounds other values in their place, can miss the bound.
Values may be sent and summed in bfloat16 or wider, within the bound.
A program may use at most 64 MiB of HBM per device.

v0:
```python
import jax
import jax.numpy as jnp
from jax import lax
from jax.sharding import PartitionSpec as P

HEAD = 128
QPG = 4


EPS = 1e-05
THETA = 1000000.0


def as_sent(shard):

    def short(part):
        return part.astype(jnp.bfloat16) if part.dtype == jnp.float32 else part

    return jax.tree.map(short, shard)


def from_partner(shard, axis, apart):
    return lax.ppermute(shard, axis, [(i, i ^ 1 << apart) for i in range(lax.axis_size(axis))])


def rotate(tensor, position):
    middle = tensor.shape[-1] // 2
    column = jnp.arange(middle, dtype=jnp.float32)
    frequency = jnp.power(THETA, -2.0 * column / tensor.shape[-1])
    angle = position * frequency
    cosine = jnp.cos(angle)
    sine = jnp.sin(angle)
    first = tensor[..., :middle]
    second = tensor[..., middle:]
    return jnp.concatenate(
        [first * cosine - second * sine, second * cosine + first * sine], axis=-1
    )


def project_rows(rows, gain, w_qkv):
    exact = lax.all_gather(rows, "tp", axis=1, tiled=True).astype(jnp.float32)
    gain_part = gain.astype(jnp.float32)
    scaled = (exact * gain_part).astype(jnp.bfloat16)
    totals = jnp.dot(scaled, w_qkv, preferred_element_type=jnp.float32)
    squares = jnp.sum(exact * exact, axis=1)
    totals, squares = (totals, squares)
    return totals * lax.rsqrt(squares / w_qkv.shape[0] + EPS)[:, None]


def split_heads(projected, position):
    groups = projected.shape[1] // ((QPG + 2) * HEAD)
    shaped = projected.reshape(projected.shape[0], groups, QPG + 2, HEAD)
    rotated = rotate(shaped, position[:, None, None, None])
    queries = rotated[:, :, :QPG].astype(jnp.bfloat16)
    keys_new = rotated[:, :, QPG].astype(jnp.bfloat16)
    values_new = shaped[:, :, QPG + 1].astype(jnp.bfloat16)
    return (queries, keys_new, values_new)


def normalize(scores):
    highest = jnp.max(scores, axis=-1, keepdims=True)
    expo = jnp.exp(scores - highest)
    return (expo / jnp.sum(expo, axis=-1, keepdims=True)).astype(jnp.bfloat16)


def block_attend(queries, keys_new, values_new, cache, offset):
    rows_count = queries.shape[0]
    groups = queries.shape[1]
    cached = cache.shape[0]
    shaped = cache.reshape(cached, groups, 2, HEAD)
    keys_all = jnp.concatenate([shaped[:, :, 0], keys_new], axis=0)
    values_all = jnp.concatenate([shaped[:, :, 1], values_new], axis=0)
    scores = jnp.einsum(
        "ckqd,jkd->kqcj", queries, keys_all, preferred_element_type=jnp.float32
    ) * HEAD ** (-0.5)
    columns = jnp.arange(cached + rows_count)[None, :]
    row_index = jnp.arange(rows_count)[:, None]
    valid = jnp.where(columns < cached, columns < offset, columns - cached <= row_index)
    scores = jnp.where(valid, scores, -jnp.inf)
    weights = normalize(scores)
    output = jnp.einsum("kqcj,jkd->ckqd", weights, values_all, preferred_element_type=jnp.float32)
    return output.reshape(rows_count, -1).astype(jnp.bfloat16)


def decode_attend(queries, keys_new, values_new, prompt, tail_cache, tail_counts):
    group_rows = queries.shape[0]
    groups = queries.shape[1]
    prompt_len = prompt.shape[0]
    tail_slots = tail_cache.shape[1]
    prompt_kv = prompt.reshape(prompt_len, groups, 2, HEAD)
    tail_kv = tail_cache.reshape(group_rows, tail_slots, groups, 2, HEAD)
    score_prompt = jnp.einsum(
        "gkqd,jkd->gkqj", queries, prompt_kv[:, :, 0], preferred_element_type=jnp.float32
    )
    score_tail = jnp.einsum(
        "gkqd,gtkd->gkqt", queries, tail_kv[:, :, :, 0], preferred_element_type=jnp.float32
    )
    live = jnp.arange(tail_slots)[None, None, None, :] < tail_counts[:, None, None, None]
    score_tail = jnp.where(live, score_tail, -jnp.inf)
    score_own = jnp.einsum("gkqd,gkd->gkq", queries, keys_new, preferred_element_type=jnp.float32)[
        ..., None
    ]
    scores = jnp.concatenate([score_prompt, score_tail, score_own], axis=-1) * HEAD ** (-0.5)
    weights = normalize(scores)
    output = jnp.einsum(
        "gkqj,jkd->gkqd",
        weights[..., :prompt_len],
        prompt_kv[:, :, 1],
        preferred_element_type=jnp.float32,
    )
    output = output + jnp.einsum(
        "gkqt,gtkd->gkqd",
        weights[..., prompt_len : prompt_len + tail_slots],
        tail_kv[:, :, :, 1],
        preferred_element_type=jnp.float32,
    )
    output = (
        output
        + weights[..., -1:].astype(jnp.float32) * values_new.astype(jnp.float32)[:, :, None, :]
    )
    return output.reshape(group_rows, -1).astype(jnp.bfloat16)


def attend_all(
    projected, block_pos, tail_counts, block_rows, ctx_cache, offset, prompt, tail_cache
):
    decode_pos = (prompt.shape[0] + tail_counts).astype(jnp.float32)
    positions = jnp.concatenate([block_pos, decode_pos], axis=0)
    queries, keys_new, values_new = split_heads(projected, positions)
    block_out = block_attend(
        queries[:block_rows], keys_new[:block_rows], values_new[:block_rows], ctx_cache, offset
    )
    decode_out = decode_attend(
        queries[block_rows:],
        keys_new[block_rows:],
        values_new[block_rows:],
        prompt,
        tail_cache,
        tail_counts,
    )
    return (block_out, decode_out)


def hop_migrate(payload, bit_index):
    return jax.tree.map(
        lambda part, own: part.astype(own.dtype),
        from_partner(as_sent(payload), "req", bit_index),
        payload,
    )


def relocate(payload, xor_mask, hop_count, mover):
    for bit_index in range(hop_count):
        take_new = jnp.bitwise_and(jnp.right_shift(xor_mask, bit_index), 1) == 1
        swapped = mover(payload, bit_index)
        payload = jax.tree.map(
            lambda stayed, arrived: jnp.where(take_new, arrived, stayed), payload, swapped
        )
    return payload


def per_device(
    block_x,
    decode_x,
    gain,
    w_qkv,
    ctx_cache,
    prompt_cache,
    tail_pool,
    page_table,
    tail_len,
    block_offset,
    move_mask,
):
    block_rows = block_x.shape[0]
    group_rows = decode_x.shape[0]
    cache_width = ctx_cache.shape[1]
    pool_pages = page_table.shape[1]
    tail_cache = jnp.take(tail_pool.reshape(pool_pages, -1, cache_width), page_table[0], axis=0)
    tail_cache = tail_cache.reshape(group_rows, -1, cache_width)
    tail_counts = tail_len[0]
    offset = block_offset[0]
    block_pos = (offset + jnp.arange(block_rows, dtype=jnp.int32)).astype(jnp.float32)
    xor_mask = move_mask[0]
    hop_count = lax.axis_size("req").bit_length() - 1
    payload = (decode_x, prompt_cache, tail_cache, tail_counts.astype(jnp.bfloat16)[None, :])
    payload = relocate(payload, xor_mask, hop_count, hop_migrate)
    moved_x, moved_prompt, moved_tails, moved_counts = payload
    projected = project_rows(jnp.concatenate([block_x, moved_x], axis=0), gain, w_qkv)
    block_out, decode_out = attend_all(
        projected,
        block_pos,
        moved_counts[0].astype(jnp.int32),
        block_rows,
        ctx_cache,
        offset,
        moved_prompt,
        moved_tails,
    )
    return (block_out, decode_out)


def solution(mesh):
    in_specs = (
        P("req", "tp"),
        P("req", "tp"),
        P(),
        P(None, "tp"),
        P("req", "tp"),
        P("req", "tp"),
        P("req", "tp"),
        P("req", None),
        P("req", None),
        P("req"),
        P(),
    )
    out_specs = (P("req", "tp"), P("req", "tp"))
    return jax.shard_map(
        per_device, mesh=mesh, in_specs=in_specs, out_specs=out_specs, check_vma=False
    )
```

profile of v0, /device:TPU:1, one launch (start us, length us, event | category | flops | bytes accessed | tf_op | source)
XLA Modules:
  0.0 409.0 jit_solution(3554118639313714812)
XLA Ops:
  7.2 8.9 %collective-permute-start = (bf16[32,512]{1,0:T(8,128)(2,1)}, bf16[32,512]{1,0:T(8,128)(2,1)S(1)}, u32[]{:S(2)}, u32[]{:S(2)}) collective-permute-start(bf16[32,512]{1,0:T(8,128)(2,1)} %param.12), channel_id=1, source_target_pairs={{0,8},{8,0},{16,24},{24,16},{32,40},{40,32},{48,56},{56,48},{64,72... | collective-permute-start | bytes 98312 | tf_op jit(solution)/shard_map/ppermute | solution.py:23
  27.2 3.1 collective-permute-start.18
  32.9 2.7 collective-permute-done.3
  35.7 2.4 collective-permute-start.4
  38.1 3.2 collective-permute-done.4
  41.9 6.9 %collective-permute-start.5 = (bf16[32,512]{1,0:T(8,128)(2,1)}, bf16[32,512]{1,0:T(8,128)(2,1)}, u32[]{:S(2)}, u32[]{:S(2)}) collective-permute-start(bf16[32,512]{1,0:T(8,128)(2,1)} %broadcast_select_fusion.16), channel_id=1, source_target_pairs={{0,256},{8,264},{16,272},{24,280},{32,288},{40,296},{48,304},{56,3... | collective-permute-start | bytes 98312 | tf_op jit(solution)/shard_map/ppermute | solution.py:23
  49.4 4.0 collective-permute-start.6
  59.3 2.7 collective-permute-start.19
  65.3 2.1 fusion.9
  67.4 18.1 %collective-permute-done.19 = bf16[32,64,256]{2,1,0:T(8,128)(2,1)} collective-permute-done((bf16[32,64,256]{2,1,0:T(8,128)(2,1)S(1)}, bf16[32,64,256]{2,1,0:T(8,128)(2,1)}, u32[]{:S(2)}, u32[]{:S(2)}) %collective-permute-start.19) | collective-permute-done | bytes 1048608 | tf_op jit(solution)/shard_map/ppermute | solution.py:23
  86.9 4.2 %collective-permute-start.20 = (bf16[32,64,256]{2,1,0:T(8,128)(2,1)S(1)}, bf16[32,64,256]{2,1,0:T(8,128)(2,1)S(1)}, u32[]{:S(2)}, u32[]{:S(2)}) collective-permute-start(bf16[32,64,256]{2,1,0:T(8,128)(2,1)S(1)} %broadcast_select_fusion.1), channel_id=1, source_target_pairs={{0,32},{8,40},{16,48},{24,56},{32,0},{40,8},{48,16},{56,24},{64,96... | collective-permute-start | bytes 3145736 | tf_op jit(solution)/shard_map/ppermute | solution.py:23
  91.2 2.2 collective-permute-start.7
  94.4 3.1 collective-permute-start.13
  97.5 15.8 %collective-permute-done.7 = bf16[1,32]{1,0:T(2,128)(2,1)S(1)} collective-permute-done((bf16[1,32]{1,0:T(2,128)(2,1)S(1)}, bf16[1,32]{1,0:T(2,128)(2,1)S(1)}, u32[]{:S(2)}, u32[]{:S(2)}) %collective-permute-start.7) | collective-permute-done | bytes 96 | tf_op jit(solution)/shard_map/ppermute | solution.py:23
  113.3 3.6 collective-permute-start.8
  117.0 2.1 collective-permute-done.8
  119.1 3.5 collective-permute-start.9
  122.7 4.1 collective-permute-start.14
  130.2 4.5 %collective-permute-start.10 = (bf16[1,32]{1,0:T(2,128)(2,1)S(1)}, bf16[1,32]{1,0:T(2,128)(2,1)S(1)}, u32[]{:S(2)}, u32[]{:S(2)}) collective-permute-start(bf16[1,32]{1,0:T(2,128)(2,1)S(1)} %broadcast_select_fusion.21), channel_id=1, source_target_pairs={{0,128},{8,136},{16,144},{24,152},{32,160},{40,168},{48,176},{56,1... | collective-permute-start | bytes 200 | tf_op jit(solution)/shard_map/ppermute | solution.py:23
  135.4 2.2 collective-permute-start.15
  137.6 74.0 %collective-permute-done.10 = bf16[1,32]{1,0:T(2,128)(2,1)S(1)} collective-permute-done((bf16[1,32]{1,0:T(2,128)(2,1)S(1)}, bf16[1,32]{1,0:T(2,128)(2,1)S(1)}, u32[]{:S(2)}, u32[]{:S(2)}) %collective-permute-start.10) | collective-permute-done | bytes 96 | tf_op jit(solution)/shard_map/ppermute | solution.py:23
  211.6 8.4 %collective-permute-start.11 = (bf16[1,32]{1,0:T(2,128)(2,1)S(1)}, bf16[1,32]{1,0:T(2,128)(2,1)S(1)}, u32[]{:S(2)}, u32[]{:S(2)}) collective-permute-start(bf16[1,32]{1,0:T(2,128)(2,1)S(1)} %broadcast_select_fusion.22), channel_id=1, source_target_pairs={{0,256},{8,264},{16,272},{24,280},{32,288},{40,296},{48,304},{56,3... | collective-permute-start | bytes 200 | tf_op jit(solution)/shard_map/ppermute | solution.py:23
  222.0 4.7 %collective-permute-start.16 = (bf16[512,256]{0,1:T(8,128)(2,1)S(1)}, bf16[512,256]{0,1:T(8,128)(2,1)S(1)}, u32[]{:S(2)}, u32[]{:S(2)}) collective-permute-start(bf16[512,256]{0,1:T(8,128)(2,1)S(1)} %broadcast_select_fusion.9), channel_id=1, source_target_pairs={{0,128},{8,136},{16,144},{24,152},{32,160},{40,168},{48,176},{56,1... | collective-permute-start | bytes 786440 | tf_op jit(solution)/shard_map/ppermute | solution.py:23
  230.5 7.6 %collective-permute-start.17 = (bf16[512,256]{0,1:T(8,128)(2,1)S(1)}, bf16[512,256]{0,1:T(8,128)(2,1)S(1)}, u32[]{:S(2)}, u32[]{:S(2)}) collective-permute-start(bf16[512,256]{0,1:T(8,128)(2,1)S(1)} %broadcast_select_fusion.10), channel_id=1, source_target_pairs={{0,256},{8,264},{16,272},{24,280},{32,288},{40,296},{48,304},{56,3... | collective-permute-start | bytes 786440 | tf_op jit(solution)/shard_map/ppermute | solution.py:23
  239.8 17.1 %collective-permute-done.17 = bf16[512,256]{0,1:T(8,128)(2,1)S(1)} collective-permute-done((bf16[512,256]{0,1:T(8,128)(2,1)S(1)}, bf16[512,256]{0,1:T(8,128)(2,1)S(1)}, u32[]{:S(2)}, u32[]{:S(2)}) %collective-permute-start.17) | collective-permute-done | bytes 262176 | tf_op jit(solution)/shard_map/ppermute | solution.py:23
  257.6 31.0 %collective-permute-done.22 = bf16[32,64,256]{2,1,0:T(8,128)(2,1)S(1)} collective-permute-done((bf16[32,64,256]{2,1,0:T(8,128)(2,1)S(1)}, bf16[32,64,256]{2,1,0:T(8,128)(2,1)S(1)}, u32[]{:S(2)}, u32[]{:S(2)}) %collective-permute-start.22) | collective-permute-done | bytes 1048608 | tf_op jit(solution)/shard_map/ppermute | solution.py:23
  289.7 6.9 %collective-permute-start.23 = (bf16[32,64,256]{2,1,0:T(8,128)(2,1)}, bf16[32,64,256]{2,1,0:T(8,128)(2,1)}, u32[]{:S(2)}, u32[]{:S(2)}) collective-permute-start(bf16[32,64,256]{2,1,0:T(8,128)(2,1)} %broadcast_select_fusion.4), channel_id=1, source_target_pairs={{0,256},{8,264},{16,272},{24,280},{32,288},{40,296},{48,304},{56,3... | collective-permute-start | bytes 3145736 | tf_op jit(solution)/shard_map/ppermute | solution.py:23
  296.6 2.7 fusion.2
  299.3 7.7 %fusion.10 = f32[416,768]{1,0:T(8,128)} fusion(bf16[4096,768]{1,0:T(8,128)(2,1)} %param.14, bf16[416,4096]{1,0:T(8,128)(2,1)} %all-gather.2.cloned.1.call-done, f32[4096]{0:T(1024)S(1)} %convert_element_type.86, f32[416]{0:T(512)S(1)} %add_rsqrt_fusion), kind=kOutput, calls=%fused_computation.16 | convolution fusion | flops 2622676992 | bytes 10995328 | tf_op jit(solution)/shard_map/dot_general | solution.py:44
  316.0 2.7 fusion.13
  319.8 76.2 %collective-permute-done.23 = bf16[32,64,256]{2,1,0:T(8,128)(2,1)} collective-permute-done((bf16[32,64,256]{2,1,0:T(8,128)(2,1)}, bf16[32,64,256]{2,1,0:T(8,128)(2,1)}, u32[]{:S(2)}, u32[]{:S(2)}) %collective-permute-start.23) | collective-permute-done | bytes 1048608 | tf_op jit(solution)/shard_map/ppermute | solution.py:23
  397.6 2.3 fusion.47
  (134 shorter events, 52.0 us)
Async XLA Ops:
  7.2 15.2 %copy-start = (bf16[2048,256]{1,0:T(8,128)(2,1)S(1)}, bf16[2048,256]{1,0:T(8,128)(2,1)}, u32[]{:S(2)}) copy-start(bf16[2048,256]{1,0:T(8,128)(2,1)} %param.17) | copy-start | bytes 3145732
  7.2 41.7 %copy-start.13 = (s32[1,32]{1,0:T(1,128)S(1)}, s32[1,32]{1,0:T(1,128)}, u32[]{:S(2)}) copy-start(s32[1,32]{1,0:T(1,128)} %param.19) | copy-start | bytes 388
  7.2 50.8 %copy-start.6 = (bf16[384,512]{1,0:T(8,128)(2,1)S(1)}, bf16[384,512]{1,0:T(8,128)(2,1)}, u32[]{:S(2)}) copy-start(bf16[384,512]{1,0:T(8,128)(2,1)} %param.11) | copy-start | bytes 1179652
  7.2 289.4 %all-gather.2.cloned.1.call-start = ((), (), s32[]{:S(2)}) async-start(), calls=%async_computation | async-start | bytes 3833856 | tf_op jit(solution)/shard_map/all_gather | solution.py:41
  7.2 12.2 %collective-permute-start = (bf16[32,512]{1,0:T(8,128)(2,1)}, bf16[32,512]{1,0:T(8,128)(2,1)S(1)}, u32[]{:S(2)}, u32[]{:S(2)}) collective-permute-start(bf16[32,512]{1,0:T(8,128)(2,1)} %param.12), channel_id=1, source_target_pairs={{0,8},{8,0},{16,24},{24,16},{32,40},{40,32},{48,56},{56,48},{64,72... | collective-permute-start | bytes 98312 | tf_op jit(solution)/shard_map/ppermute | solution.py:23
  20.2 4.6 %collective-permute-start.1 = (bf16[32,512]{1,0:T(8,128)(2,1)S(1)}, bf16[32,512]{1,0:T(8,128)(2,1)S(1)}, u32[]{:S(2)}, u32[]{:S(2)}) collective-permute-start(bf16[32,512]{1,0:T(8,128)(2,1)S(1)} %broadcast_select_fusion.12), channel_id=1, source_target_pairs={{0,16},{8,24},{16,0},{24,8},{32,48},{40,56},{48,32},{56,40},{64,80... | collective-permute-start | bytes 98312 | tf_op jit(solution)/shard_map/ppermute | solution.py:23
  24.8 6.2 %collective-permute-start.2 = (bf16[32,512]{1,0:T(8,128)(2,1)S(1)}, bf16[32,512]{1,0:T(8,128)(2,1)S(1)}, u32[]{:S(2)}, u32[]{:S(2)}) collective-permute-start(bf16[32,512]{1,0:T(8,128)(2,1)S(1)} %broadcast_select_fusion.13), channel_id=1, source_target_pairs={{0,32},{8,40},{16,48},{24,56},{32,0},{40,8},{48,16},{56,24},{64,96... | collective-permute-start | bytes 98312 | tf_op jit(solution)/shard_map/ppermute | solution.py:23
  27.2 31.6 %collective-permute-start.18 = (bf16[32,64,256]{2,1,0:T(8,128)(2,1)S(1)}, bf16[32,64,256]{2,1,0:T(8,128)(2,1)}, u32[]{:S(2)}, u32[]{:S(2)}) collective-permute-start(bf16[32,64,256]{2,1,0:T(8,128)(2,1)S(1)} %bitcast_select_fusion.1), channel_id=1, source_target_pairs={{0,8},{8,0},{16,24},{24,16},{32,40},{40,32},{48,56},{56,48},{64,72... | collective-permute-start | bytes 3145736 | tf_op jit(solution)/shard_map/ppermute | solution.py:23
  31.0 4.7 %collective-permute-start.3 = (bf16[32,512]{1,0:T(8,128)(2,1)S(1)}, bf16[32,512]{1,0:T(8,128)(2,1)S(1)}, u32[]{:S(2)}, u32[]{:S(2)}) collective-permute-start(bf16[32,512]{1,0:T(8,128)(2,1)S(1)} %broadcast_select_fusion.14), channel_id=1, source_target_pairs={{0,64},{8,72},{16,80},{24,88},{32,96},{40,104},{48,112},{56,120},{... | collective-permute-start | bytes 98312 | tf_op jit(solution)/shard_map/ppermute | solution.py:23
  35.7 5.6 %collective-permute-start.4 = (bf16[32,512]{1,0:T(8,128)(2,1)S(1)}, bf16[32,512]{1,0:T(8,128)(2,1)S(1)}, u32[]{:S(2)}, u32[]{:S(2)}) collective-permute-start(bf16[32,512]{1,0:T(8,128)(2,1)S(1)} %broadcast_select_fusion.15), channel_id=1, source_target_pairs={{0,128},{8,136},{16,144},{24,152},{32,160},{40,168},{48,176},{56,1... | collective-permute-start | bytes 98312 | tf_op jit(solution)/shard_map/ppermute | solution.py:23
  41.9 15.3 %collective-permute-start.5 = (bf16[32,512]{1,0:T(8,128)(2,1)}, bf16[32,512]{1,0:T(8,128)(2,1)}, u32[]{:S(2)}, u32[]{:S(2)}) collective-permute-start(bf16[32,512]{1,0:T(8,128)(2,1)} %broadcast_select_fusion.16), channel_id=1, source_target_pairs={{0,256},{8,264},{16,272},{24,280},{32,288},{40,296},{48,304},{56,3... | collective-permute-start | bytes 98312 | tf_op jit(solution)/shard_map/ppermute | solution.py:23
  49.4 41.7 %collective-permute-start.6 = (bf16[1,32]{1,0:T(2,128)(2,1)}, bf16[1,32]{1,0:T(2,128)(2,1)}, u32[]{:S(2)}, u32[]{:S(2)}) collective-permute-start(bf16[1,32]{1,0:T(2,128)(2,1)} %convert_element_type.89), channel_id=1, source_target_pairs={{0,8},{8,0},{16,24},{24,16},{32,40},{40,32},{48,56},{56,48},{64,72... | collective-permute-start | bytes 200 | tf_op jit(solution)/shard_map/ppermute | solution.py:23
  55.3 38.1 %collective-permute-start.12 = (bf16[512,256]{0,1:T(8,128)(2,1)}, bf16[512,256]{0,1:T(8,128)(2,1)}, u32[]{:S(2)}, u32[]{:S(2)}) collective-permute-start(bf16[512,256]{0,1:T(8,128)(2,1)} %copy.30), channel_id=1, source_target_pairs={{0,8},{8,0},{16,24},{24,16},{32,40},{40,32},{48,56},{56,48},{64,72... | collective-permute-start | bytes 786440 | tf_op jit(solution)/shard_map/ppermute | solution.py:23
  58.8 58.2 %copy-start.11 = (bf16[4096]{0:T(1024)(128)(2,1)S(1)}, bf16[4096]{0:T(1024)(128)(2,1)}, u32[]{:S(2)}) copy-start(bf16[4096]{0:T(1024)(128)(2,1)} %param.13) | copy-start | bytes 24580
  59.3 31.8 %copy-start.14 = (s32[1,32]{1,0:T(1,128)S(1)}, s32[1,32]{1,0:T(1,128)}, u32[]{:S(2)}) copy-start(s32[1,32]{1,0:T(1,128)} %param.19) | copy-start | bytes 388
  59.3 26.2 %collective-permute-start.19 = (bf16[32,64,256]{2,1,0:T(8,128)(2,1)S(1)}, bf16[32,64,256]{2,1,0:T(8,128)(2,1)}, u32[]{:S(2)}, u32[]{:S(2)}) collective-permute-start(bf16[32,64,256]{2,1,0:T(8,128)(2,1)S(1)} %broadcast_select_fusion), channel_id=1, source_target_pairs={{0,16},{8,24},{16,0},{24,8},{32,48},{40,56},{48,32},{56,40},{64,80... | collective-permute-start | bytes 3145736 | tf_op jit(solution)/shard_map/ppermute | solution.py:23
  86.9 40.0 %collective-permute-start.20 = (bf16[32,64,256]{2,1,0:T(8,128)(2,1)S(1)}, bf16[32,64,256]{2,1,0:T(8,128)(2,1)S(1)}, u32[]{:S(2)}, u32[]{:S(2)}) collective-permute-start(bf16[32,64,256]{2,1,0:T(8,128)(2,1)S(1)} %broadcast_select_fusion.1), channel_id=1, source_target_pairs={{0,32},{8,40},{16,48},{24,56},{32,0},{40,8},{48,16},{56,24},{64,96... | collective-permute-start | bytes 3145736 | tf_op jit(solution)/shard_map/ppermute | solution.py:23
  91.2 22.2 %collective-permute-start.7 = (bf16[1,32]{1,0:T(2,128)(2,1)S(1)}, bf16[1,32]{1,0:T(2,128)(2,1)S(1)}, u32[]{:S(2)}, u32[]{:S(2)}) collective-permute-start(bf16[1,32]{1,0:T(2,128)(2,1)S(1)} %broadcast_select_fusion.18), channel_id=1, source_target_pairs={{0,16},{8,24},{16,0},{24,8},{32,48},{40,56},{48,32},{56,40},{64,80... | collective-permute-start | bytes 200 | tf_op jit(solution)/shard_map/ppermute | solution.py:23
  94.4 28.3 %collective-permute-start.13 = (bf16[512,256]{0,1:T(8,128)(2,1)S(1)}, bf16[512,256]{0,1:T(8,128)(2,1)S(1)}, u32[]{:S(2)}, u32[]{:S(2)}) collective-permute-start(bf16[512,256]{0,1:T(8,128)(2,1)S(1)} %broadcast_select_fusion.6), channel_id=1, source_target_pairs={{0,16},{8,24},{16,0},{24,8},{32,48},{40,56},{48,32},{56,40},{64,80... | collective-permute-start | bytes 786440 | tf_op jit(solution)/shard_map/ppermute | solution.py:23
  113.3 5.8 %collective-permute-start.8 = (bf16[1,32]{1,0:T(2,128)(2,1)S(1)}, bf16[1,32]{1,0:T(2,128)(2,1)S(1)}, u32[]{:S(2)}, u32[]{:S(2)}) collective-permute-start(bf16[1,32]{1,0:T(2,128)(2,1)S(1)} %broadcast_select_fusion.19), channel_id=1, source_target_pairs={{0,32},{8,40},{16,48},{24,56},{32,0},{40,8},{48,16},{56,24},{64,96... | collective-permute-start | bytes 200 | tf_op jit(solution)/shard_map/ppermute | solution.py:23
  119.1 11.0 %collective-permute-start.9 = (bf16[1,32]{1,0:T(2,128)(2,1)S(1)}, bf16[1,32]{1,0:T(2,128)(2,1)S(1)}, u32[]{:S(2)}, u32[]{:S(2)}) collective-permute-start(bf16[1,32]{1,0:T(2,128)(2,1)S(1)} %broadcast_select_fusion.20), channel_id=1, source_target_pairs={{0,64},{8,72},{16,80},{24,88},{32,96},{40,104},{48,112},{56,120},{... | collective-permute-start | bytes 200 | tf_op jit(solution)/shard_map/ppermute | solution.py:23
  122.7 115.4 %copy-start.12 = (f32[64]{0:T(128)S(1)}, f32[64]{0:T(128)}, u32[]{:S(2)}) copy-start(f32[64]{0:T(128)} %multiply_power_fusion) | copy-start | bytes 772
  122.7 11.9 %collective-permute-start.14 = (bf16[512,256]{0,1:T(8,128)(2,1)S(1)}, bf16[512,256]{0,1:T(8,128)(2,1)S(1)}, u32[]{:S(2)}, u32[]{:S(2)}) collective-permute-start(bf16[512,256]{0,1:T(8,128)(2,1)S(1)} %broadcast_select_fusion.7), channel_id=1, source_target_pairs={{0,32},{8,40},{16,48},{24,56},{32,0},{40,8},{48,16},{56,24},{64,96... | collective-permute-start | bytes 786440 | tf_op jit(solution)/shard_map/ppermute | solution.py:23
  127.0 99.7 %collective-permute-start.21 = (bf16[32,64,256]{2,1,0:T(8,128)(2,1)S(1)}, bf16[32,64,256]{2,1,0:T(8,128)(2,1)S(1)}, u32[]{:S(2)}, u32[]{:S(2)}) collective-permute-start(bf16[32,64,256]{2,1,0:T(8,128)(2,1)S(1)} %broadcast_select_fusion.2), channel_id=1, source_target_pairs={{0,64},{8,72},{16,80},{24,88},{32,96},{40,104},{48,112},{56,120},{... | collective-permute-start | bytes 3145736 | tf_op jit(solution)/shard_map/ppermute | solution.py:23
  130.2 81.4 %collective-permute-start.10 = (bf16[1,32]{1,0:T(2,128)(2,1)S(1)}, bf16[1,32]{1,0:T(2,128)(2,1)S(1)}, u32[]{:S(2)}, u32[]{:S(2)}) collective-permute-start(bf16[1,32]{1,0:T(2,128)(2,1)S(1)} %broadcast_select_fusion.21), channel_id=1, source_target_pairs={{0,128},{8,136},{16,144},{24,152},{32,160},{40,168},{48,176},{56,1... | collective-permute-start | bytes 200 | tf_op jit(solution)/shard_map/ppermute | solution.py:23
  135.4 85.6 %collective-permute-start.15 = (bf16[512,256]{0,1:T(8,128)(2,1)}, bf16[512,256]{0,1:T(8,128)(2,1)}, u32[]{:S(2)}, u32[]{:S(2)}) collective-permute-start(bf16[512,256]{0,1:T(8,128)(2,1)} %broadcast_select_fusion.8), channel_id=1, source_target_pairs={{0,64},{8,72},{16,80},{24,88},{32,96},{40,104},{48,112},{56,120},{... | collective-permute-start | bytes 786440 | tf_op jit(solution)/shard_map/ppermute | solution.py:23
  211.6 9.4 %collective-permute-start.11 = (bf16[1,32]{1,0:T(2,128)(2,1)S(1)}, bf16[1,32]{1,0:T(2,128)(2,1)S(1)}, u32[]{:S(2)}, u32[]{:S(2)}) collective-permute-start(bf16[1,32]{1,0:T(2,128)(2,1)S(1)} %broadcast_select_fusion.22), channel_id=1, source_target_pairs={{0,256},{8,264},{16,272},{24,280},{32,288},{40,296},{48,304},{56,3... | collective-permute-start | bytes 200 | tf_op jit(solution)/shard_map/ppermute | solution.py:23
  222.0 8.4 %collective-permute-start.16 = (bf16[512,256]{0,1:T(8,128)(2,1)S(1)}, bf16[512,256]{0,1:T(8,128)(2,1)S(1)}, u32[]{:S(2)}, u32[]{:S(2)}) collective-permute-start(bf16[512,256]{0,1:T(8,128)(2,1)S(1)} %broadcast_select_fusion.9), channel_id=1, source_target_pairs={{0,128},{8,136},{16,144},{24,152},{32,160},{40,168},{48,176},{56,1... | collective-permute-start | bytes 786440 | tf_op jit(solution)/shard_map/ppermute | solution.py:23
  226.8 61.7 %collective-permute-start.22 = (bf16[32,64,256]{2,1,0:T(8,128)(2,1)S(1)}, bf16[32,64,256]{2,1,0:T(8,128)(2,1)S(1)}, u32[]{:S(2)}, u32[]{:S(2)}) collective-permute-start(bf16[32,64,256]{2,1,0:T(8,128)(2,1)S(1)} %broadcast_select_fusion.3), channel_id=1, source_target_pairs={{0,128},{8,136},{16,144},{24,152},{32,160},{40,168},{48,176},{56,1... | collective-permute-start | bytes 3145736 | tf_op jit(solution)/shard_map/ppermute | solution.py:23
  230.5 26.4 %collective-permute-start.17 = (bf16[512,256]{0,1:T(8,128)(2,1)S(1)}, bf16[512,256]{0,1:T(8,128)(2,1)S(1)}, u32[]{:S(2)}, u32[]{:S(2)}) collective-permute-start(bf16[512,256]{0,1:T(8,128)(2,1)S(1)} %broadcast_select_fusion.10), channel_id=1, source_target_pairs={{0,256},{8,264},{16,272},{24,280},{32,288},{40,296},{48,304},{56,3... | collective-permute-start | bytes 786440 | tf_op jit(solution)/shard_map/ppermute | solution.py:23
  289.7 106.3 %collective-permute-start.23 = (bf16[32,64,256]{2,1,0:T(8,128)(2,1)}, bf16[32,64,256]{2,1,0:T(8,128)(2,1)}, u32[]{:S(2)}, u32[]{:S(2)}) collective-permute-start(bf16[32,64,256]{2,1,0:T(8,128)(2,1)} %broadcast_select_fusion.4), channel_id=1, source_target_pairs={{0,256},{8,264},{16,272},{24,280},{32,288},{40,296},{48,304},{56,3... | collective-permute-start | bytes 3145736 | tf_op jit(solution)/shard_map/ppermute | solution.py:23
  397.6 3.7 copy-start.5
  (8 other events, 14.4 us)
Sparse Core Ops, SparseCore 0:
  58.9 154.5 all-gather.1
where the time goes:
time: 410 us; the launch traced here: 409 us
  waiting for transfers between devices  246 us (60%)
  starting transfers between devices  94.6 us (23%)
  other arithmetic  25.5 us (6%)
  between operations  16.1 us (4%)
  local copies, waits for them, and re-layouts  13.9 us (3%)
  matrix products  13 us (3%)
    ppermute x24, waiting for transfers between devices, from_partner(): lax.ppermute(shard, axis, [(i, i ^ 1 << apart) for i in range(lax.axis_si...  246 us
    ppermute x24, starting transfers between devices, from_partner(): lax.ppermute(shard, axis, [(i, i ^ 1 << apart) for i in range(lax.axis_si...  94.6 us
    select_n x23, other arithmetic, relocate(): jnp.where(take_new, arrived, stayed)  10.3 us
  transfers between devices with their start and end apart: 25, of which 14 were waited for; matrix products, arithmetic and copies ran while one was open for 11% of the time, Pallas kernels for 0%

commit v1 on v0

--- a/solution.py
+++ b/solution.py
@@ -183,20 +183,18 @@
     block_pos = (offset + jnp.arange(block_rows, dtype=jnp.int32)).astype(jnp.float32)
     xor_mask = move_mask[0]
     hop_count = lax.axis_size("req").bit_length() - 1
-    payload = (decode_x, prompt_cache, tail_cache, tail_counts.astype(jnp.bfloat16)[None, :])
-    payload = relocate(payload, xor_mask, hop_count, hop_migrate)
-    moved_x, moved_prompt, moved_tails, moved_counts = payload
-    projected = project_rows(jnp.concatenate([block_x, moved_x], axis=0), gain, w_qkv)
+    projected = project_rows(jnp.concatenate([block_x, decode_x], axis=0), gain, w_qkv)
     block_out, decode_out = attend_all(
         projected,
         block_pos,
-        moved_counts[0].astype(jnp.int32),
+        tail_counts,
         block_rows,
         ctx_cache,
         offset,
-        moved_prompt,
-        moved_tails,
-    )
+        prompt_cache,
+        tail_cache,
+    )
+    decode_out = relocate(decode_out, xor_mask, hop_count, hop_migrate)
     return (block_out, decode_out)
 
 

time: 410 us -> 239 us (0.58)
  the two profiles are of different devices: /device:TPU:1 before, /device:TPU:2 now
where the time goes in v1:
time: 239 us
  waiting for transfers between devices  149 us (62%)
  starting transfers between devices  29.5 us (12%)
  other arithmetic  16.9 us (7%)
  between operations  15.7 us (7%)
  matrix products  14.9 us (6%)
  local copies, waits for them, and re-layouts  12.9 us (5%)
    all_gather x1, waiting for transfers between devices, project_rows(): exact = lax.all_gather(rows, 'tp', axis=1, tiled=True).astype(jnp.float32)  139 us
    ppermute x6, starting transfers between devices, from_partner(): lax.ppermute(shard, axis, [(i, i ^ 1 << apart) for i in range(lax.axis_si...  29.5 us
    ppermute x6, waiting for transfers between devices, from_partner(): lax.ppermute(shard, axis, [(i, i ^ 1 << apart) for i in range(lax.axis_si...  10.1 us
    dot_general x1, matrix products, project_rows(): totals = jnp.dot(scaled, w_qkv, preferred_element_type=jnp.float32)  7.69 us
    unnamed x26, local copies, waits for them, and re-layouts  6.36 us
  transfers between devices with their start and end apart: 7, of which 7 were waited for; matrix products, arithmetic and copies ran while one was open for 9% of the time, Pallas kernels for 0%

profile of v1, /device:TPU:2, one launch (start us, length us, event | category | flops | bytes accessed | tf_op | source)
XLA Modules:
  0.0 238.7 jit_solution(3643372423016336073)
XLA Ops:
  7.2 1.9 pad_maximum_fusion
  11.0 1.3 reduce.9
  13.3 1.8 copy.30
  15.1 1.2 copy.24
  17.1 0.8 copy.47
  19.1 1.6 multiply_cosine_fusion
  20.7 1.3 copy_select_fusion
  22.0 2.1 fusion.9
  24.1 138.7 %all-gather.2.cloned.1.call-done = bf16[416,4096]{1,0:T(8,128)(2,1)} async-done(((bf16[416,512]{1,0:T(8,128)(2,1)}), bf16[416,4096]{1,0:T(8,128)(2,1)}) %all-gather.2.cloned.1.call-update) | async-done | bytes 3407888 | tf_op jit(solution)/shard_map/all_gather | solution.py:41
  162.9 2.7 %fusion.2 = f32[416]{0:T(512)S(1)} fusion(bf16[416,4096]{1,0:T(8,128)(2,1)} %all-gather.2.cloned.1.call-done), kind=kLoop, calls=%fused_computation.8 | loop fusion | flops 5111392 | bytes 3409536 | tf_op jit(solution)/shard_map/reduce_sum | solution.py:45
  165.6 7.7 %fusion.10 = f32[416,768]{1,0:T(8,128)} fusion(bf16[4096,768]{1,0:T(8,128)(2,1)} %param.14, bf16[416,4096]{1,0:T(8,128)(2,1)} %all-gather.2.cloned.1.call-done, f32[4096]{0:T(1024)S(1)} %convert_element_type.72, f32[416]{0:T(512)S(1)} %add_rsqrt_fusion), kind=kOutput, calls=%fused_computation.16 | convolution fusion | flops 2622676992 | bytes 10995328 | tf_op jit(solution)/shard_map/dot_general | solution.py:44
  173.3 1.4 reshape.431
  174.7 1.5 copy.25
  178.6 1.1 convolution_bitcast_fusion
  182.0 1.2 fusion.18
  183.2 1.9 collective-permute-start
  185.5 0.8 collective-permute-done
  186.3 6.3 %collective-permute-start.1 = (bf16[32,512]{1,0:T(8,128)(2,1)S(1)}, bf16[32,512]{1,0:T(8,128)(2,1)S(1)}, u32[]{:S(2)}, u32[]{:S(2)}) collective-permute-start(bf16[32,512]{1,0:T(8,128)(2,1)S(1)} %broadcast_select_fusion), channel_id=1, source_target_pairs={{0,16},{8,24},{16,0},{24,8},{32,48},{40,56},{48,32},{56,40},{64,80... | collective-permute-start | bytes 98312 | tf_op jit(solution)/shard_map/ppermute | solution.py:23
  192.7 1.8 collective-permute-done.1
  194.5 1.9 collective-permute-start.2
  196.4 1.5 fusion.3
  197.9 3.9 %collective-permute-done.2 = bf16[32,512]{1,0:T(8,128)(2,1)S(1)} collective-permute-done((bf16[32,512]{1,0:T(8,128)(2,1)S(1)}, bf16[32,512]{1,0:T(8,128)(2,1)S(1)}, u32[]{:S(2)}, u32[]{:S(2)}) %collective-permute-start.2) | collective-permute-done | bytes 32800 | tf_op jit(solution)/shard_map/ppermute | solution.py:23
  201.8 2.9 %collective-permute-start.3 = (bf16[32,512]{1,0:T(8,128)(2,1)S(1)}, bf16[32,512]{1,0:T(8,128)(2,1)S(1)}, u32[]{:S(2)}, u32[]{:S(2)}) collective-permute-start(bf16[32,512]{1,0:T(8,128)(2,1)S(1)} %broadcast_select_fusion.2), channel_id=1, source_target_pairs={{0,64},{8,72},{16,80},{24,88},{32,96},{40,104},{48,112},{56,120},{... | collective-permute-start | bytes 98312 | tf_op jit(solution)/shard_map/ppermute | solution.py:23
  204.7 1.8 fusion
  206.5 1.1 collective-permute-done.3
  207.6 12.0 %collective-permute-start.4 = (bf16[32,512]{1,0:T(8,128)(2,1)S(1)}, bf16[32,512]{1,0:T(8,128)(2,1)S(1)}, u32[]{:S(2)}, u32[]{:S(2)}) collective-permute-start(bf16[32,512]{1,0:T(8,128)(2,1)S(1)} %broadcast_select_fusion.3), channel_id=1, source_target_pairs={{0,128},{8,136},{16,144},{24,152},{32,160},{40,168},{48,176},{56,1... | collective-permute-start | bytes 98312 | tf_op jit(solution)/shard_map/ppermute | solution.py:23
  219.6 0.9 slice_bitcast_fusion.13
  220.5 1.0 collective-permute-done.4
  221.5 4.5 %collective-permute-start.5 = (bf16[32,512]{1,0:T(8,128)(2,1)S(1)}, bf16[32,512]{1,0:T(8,128)(2,1)S(1)}, u32[]{:S(2)}, u32[]{:S(2)}) collective-permute-start(bf16[32,512]{1,0:T(8,128)(2,1)S(1)} %broadcast_select_fusion.4), channel_id=1, source_target_pairs={{0,256},{8,264},{16,272},{24,280},{32,288},{40,296},{48,304},{56,3... | collective-permute-start | bytes 98312 | tf_op jit(solution)/shard_map/ppermute | solution.py:23
  226.0 2.7 %fusion.13 = bf16[128,4,384]{2,0,1:T(8,128)(2,1)S(1)} fusion(f32[4,384]{1,0:T(4,128)S(1)} %fusion, f32[4,384]{1,0:T(4,128)S(1)} %get-tuple-element.14, f32[1408,384,4]{1,0,2:T(8,128)S(1)} %get-tuple-element.15, pred[384,1408]{0,1:T(8,128)(4,1)S(1)} %copy-done.2, bf16[384,1,128]{0,2,1:T(8,128)(2,1)S(1)} %slice_bitcast_fusion.13, ...), kind=kOutput, calls=%fused_computation.20 | convolution fusion | flops 565379072 | bytes 9957376 | tf_op jit(solution)/shard_map/kqcj,jkd->ckqd/dot_general | solution.py:81
  228.7 0.9 copy.43
  229.7 1.6 collective-permute-done.5
  (69 shorter events, 9.2 us)
Async XLA Ops:
  7.2 10.8 %copy-start = (bf16[2048,256]{1,0:T(8,128)(2,1)S(1)}, bf16[2048,256]{1,0:T(8,128)(2,1)}, u32[]{:S(2)}) copy-start(bf16[2048,256]{1,0:T(8,128)(2,1)} %param.17) | copy-start | bytes 3145732
  7.2 10.8 %copy-start.9 = (s32[1,128]{1,0:T(1,128)S(1)}, s32[1,128]{1,0:T(1,128)}, u32[]{:S(2)}) copy-start(s32[1,128]{1,0:T(1,128)} %param.18) | copy-start | bytes 1540
  7.2 11.8 %copy-start.8 = (s32[1,32]{1,0:T(1,128)S(1)}, s32[1,32]{1,0:T(1,128)}, u32[]{:S(2)}) copy-start(s32[1,32]{1,0:T(1,128)} %param.19) | copy-start | bytes 388
  7.2 155.6 %all-gather.2.cloned.1.call-start = ((), (), s32[]{:S(2)}) async-start(), calls=%async_computation | async-start | bytes 3833856 | tf_op jit(solution)/shard_map/all_gather | solution.py:41
  176.1 0.9 copy-start.3
  176.1 1.0 copy-start.4
  176.7 1.5 copy-start.1
  180.2 0.7 copy-start.5
  181.7 14.7 %copy-start.2 = (pred[384,1408]{0,1:T(8,128)(4,1)S(1)}, pred[384,1408]{0,1:T(8,128)(4,1)}, u32[]{:S(2)}) copy-start(pred[384,1408]{0,1:T(8,128)(4,1)} %fusion.9) | copy-start | bytes 1622020
  181.7 14.7 %copy-start.6 = (bf16[1024,1,1,128]{3,0,2,1:T(8,128)(2,1)S(1)}, bf16[1024,1,1,128]{3,0,2,1:T(8,128)(2,1)}, u32[]{:S(2)}) copy-start(bf16[1024,1,1,128]{3,0,2,1:T(8,128)(2,1)} %copy.47) | copy-start | bytes 786436
  183.2 3.1 %collective-permute-start = (bf16[32,512]{1,0:T(8,128)(2,1)S(1)}, bf16[32,512]{1,0:T(8,128)(2,1)S(1)}, u32[]{:S(2)}, u32[]{:S(2)}) collective-permute-start(bf16[32,512]{1,0:T(8,128)(2,1)S(1)} %bitcast.139), channel_id=1, source_target_pairs={{0,8},{8,0},{16,24},{24,16},{32,40},{40,32},{48,56},{56,48},{64,72... | collective-permute-start | bytes 98312 | tf_op jit(solution)/shard_map/ppermute | solution.py:23
  186.3 8.1 %collective-permute-start.1 = (bf16[32,512]{1,0:T(8,128)(2,1)S(1)}, bf16[32,512]{1,0:T(8,128)(2,1)S(1)}, u32[]{:S(2)}, u32[]{:S(2)}) collective-permute-start(bf16[32,512]{1,0:T(8,128)(2,1)S(1)} %broadcast_select_fusion), channel_id=1, source_target_pairs={{0,16},{8,24},{16,0},{24,8},{32,48},{40,56},{48,32},{56,40},{64,80... | collective-permute-start | bytes 98312 | tf_op jit(solution)/shard_map/ppermute | solution.py:23
  194.5 7.3 %collective-permute-start.2 = (bf16[32,512]{1,0:T(8,128)(2,1)S(1)}, bf16[32,512]{1,0:T(8,128)(2,1)S(1)}, u32[]{:S(2)}, u32[]{:S(2)}) collective-permute-start(bf16[32,512]{1,0:T(8,128)(2,1)S(1)} %broadcast_select_fusion.1), channel_id=1, source_target_pairs={{0,32},{8,40},{16,48},{24,56},{32,0},{40,8},{48,16},{56,24},{64,96... | collective-permute-start | bytes 98312 | tf_op jit(solution)/shard_map/ppermute | solution.py:23
  201.8 5.8 %collective-permute-start.3 = (bf16[32,512]{1,0:T(8,128)(2,1)S(1)}, bf16[32,512]{1,0:T(8,128)(2,1)S(1)}, u32[]{:S(2)}, u32[]{:S(2)}) collective-permute-start(bf16[32,512]{1,0:T(8,128)(2,1)S(1)} %broadcast_select_fusion.2), channel_id=1, source_target_pairs={{0,64},{8,72},{16,80},{24,88},{32,96},{40,104},{48,112},{56,120},{... | collective-permute-start | bytes 98312 | tf_op jit(solution)/shard_map/ppermute | solution.py:23
  204.7 21.4 %copy-start.7 = (bf16[1024,1,128]{0,2,1:T(8,128)(2,1)S(1)}, bf16[1024,1,128]{0,2,1:T(8,128)(2,1)}, u32[]{:S(2)}) copy-start(bf16[1024,1,128]{0,2,1:T(8,128)(2,1)} %get-tuple-element.10) | copy-start | bytes 786436
  207.6 13.9 %collective-permute-start.4 = (bf16[32,512]{1,0:T(8,128)(2,1)S(1)}, bf16[32,512]{1,0:T(8,128)(2,1)S(1)}, u32[]{:S(2)}, u32[]{:S(2)}) collective-permute-start(bf16[32,512]{1,0:T(8,128)(2,1)S(1)} %broadcast_select_fusion.3), channel_id=1, source_target_pairs={{0,128},{8,136},{16,144},{24,152},{32,160},{40,168},{48,176},{56,1... | collective-permute-start | bytes 98312 | tf_op jit(solution)/shard_map/ppermute | solution.py:23
  221.5 9.7 %collective-permute-start.5 = (bf16[32,512]{1,0:T(8,128)(2,1)S(1)}, bf16[32,512]{1,0:T(8,128)(2,1)S(1)}, u32[]{:S(2)}, u32[]{:S(2)}) collective-permute-start(bf16[32,512]{1,0:T(8,128)(2,1)S(1)} %broadcast_select_fusion.4), channel_id=1, source_target_pairs={{0,256},{8,264},{16,272},{24,280},{32,288},{40,296},{48,304},{56,3... | collective-permute-start | bytes 98312 | tf_op jit(solution)/shard_map/ppermute | solution.py:23
Sparse Core Ops, SparseCore 0:
  11.1 151.7 all-gather.1

commit v2 on v1

v2 whole, which is shorter than its diff:
```python
import functools
import math

import jax
import jax.numpy as jnp
import numpy as np
from jax import lax
from jax.experimental import pallas as pl
from jax.experimental.pallas import tpu as pltpu
from jax.sharding import PartitionSpec as P

HEAD = 128
QPG = 4
EPS = 1e-05
THETA = 1000000.0
PAGE = 16
MESH = pl.DeviceIdType.MESH
CHUNKS = ((0, 32), (32, 96), (128, 96), (224, 96), (320, 64), (384, 32))
OWN = ((0, 32), (32, 192), (224, 192))
HOPS = 6
MASKED = -1e30
FACTOR = HEAD ** -0.5 * math.log2(math.e)


def where_am_i():
    req = lax.axis_index("req")
    tp = lax.axis_index("tp")
    return req, tp, tp // 2, tp % 2


def layer_kernel(
    block_x, decode_x, gain, w_hbm, ctx_hbm, prompt_hbm, pool_hbm, table, tail_len, offset, mask, freq,
    block_out, decode_out,
    gathered, w, ctx, prompt, pool, place_of, acc, squares, cosines, sines, keys_new, values_new,
    out_rows, moved, landed, local_sem, send_sem, recv_sem,
):
    req, tp, y, zh = where_am_i()
    group_rows = decode_x.shape[0]
    block_rows = block_x.shape[0]
    depth = decode_x.shape[1]
    opposite = (req, tp + 1 - 2 * zh)

    def along_y(step):
        return (req, ((y + step + 4) % 4) * 2 + zh)

    def partner(bit):
        here = (req // (1 << bit)) % 2
        return (req + (1 - 2 * here) * (1 << bit), tp)

    peers = [opposite, along_y(1), along_y(-1)] + [partner(bit) for bit in range(HOPS)]
    barrier = pltpu.get_barrier_semaphore()
    for peer in peers:
        pl.semaphore_signal(barrier, inc=1, device_id=peer, device_id_type=MESH)

    locals_ = [
        pltpu.make_async_copy(decode_x, gathered.at[tp, pl.ds(0, group_rows)], local_sem.at[0]),
        pltpu.make_async_copy(block_x, gathered.at[tp, pl.ds(group_rows, block_rows)], local_sem.at[1]),
        pltpu.make_async_copy(w_hbm, w, local_sem.at[2]),
        pltpu.make_async_copy(pool_hbm, pool, local_sem.at[3]),
        pltpu.make_async_copy(prompt_hbm, prompt, local_sem.at[4]),
        pltpu.make_async_copy(ctx_hbm, ctx, local_sem.at[5]),
    ]
    for copy in locals_:
        copy.start()
    pl.semaphore_wait(barrier, len(peers))

    sent = []

    def send(source, target, device):
        index = len(sent)
        copy = pltpu.make_async_remote_copy(
            src_ref=source, dst_ref=target, send_sem=send_sem.at[index], recv_sem=recv_sem.at[index],
            device_id=device, device_id_type=MESH,
        )
        copy.start()
        sent.append(copy)
        return copy

    def own_rows(start, rows):
        if start < group_rows:
            return decode_x.at[pl.ds(start, rows)]
        return block_x.at[pl.ds(start - group_rows, rows)]

    directions = (1, -1)
    across = [send(own_rows(s, n), gathered.at[tp, pl.ds(s, n)], opposite) for s, n in CHUNKS]
    beside = [
        [send(own_rows(s, n), gathered.at[tp, pl.ds(s, n)], along_y(d)) for d in directions] for s, n in OWN
    ]

    def forward(arrived, start, rows, half):
        copies = []
        for which, d in enumerate(directions):
            arrived[which].wait_recv()
            slot = ((y - d + 4) % 4) * 2 + half
            view = gathered.at[slot, pl.ds(start + which * (rows // 2), rows // 2)]
            copies.append(send(view, view, along_y(d)))
        return copies

    def forward_own(index):
        return forward(beside[index], OWN[index][0], OWN[index][1], zh)

    def spread(index):
        start, rows = CHUNKS[index]
        across[index].wait_recv()
        view = gathered.at[tp + 1 - 2 * zh, pl.ds(start, rows)]
        return [send(view, view, along_y(d)) for d in directions]

    def forward_far(index, arrived):
        return forward(arrived, CHUNKS[index][0], CHUNKS[index][1], 1 - zh)

    def half_product(start, rows, half):
        total = None
        square = None
        for j in range(4):
            slot = 2 * j + half
            exact = gathered[slot, pl.ds(start, rows), :].astype(jnp.float32)
            base = pl.multiple_of(slot * depth, depth)
            scaled = (exact * gain[:, pl.ds(base, depth)]).astype(jnp.bfloat16)
            term = jnp.dot(scaled, w[pl.ds(base, depth), :], preferred_element_type=jnp.float32)
            total = term if total is None else total + term
            exact = exact * exact
            folded = (exact[:, :128] + exact[:, 128:256]) + (exact[:, 256:384] + exact[:, 384:512])
            square = folded if square is None else square + folded
        return total, square

    def early_half(start, rows):
        total, square = half_product(start, rows, zh)
        acc[pl.ds(start, rows), :] = total
        squares[pl.ds(start, rows), :] = square

    def project(start, rows):
        total, square = half_product(start, rows, 1 - zh)
        total = total + acc[pl.ds(start, rows), :]
        square = jnp.sum(square + squares[pl.ds(start, rows), :], axis=1, keepdims=True)
        projected = total * lax.rsqrt(square / (8 * depth) + EPS)
        cosine = cosines[pl.ds(start, rows), :]
        sine = sines[pl.ds(start, rows), :]

        def head(index):
            return projected[:, index * HEAD : (index + 1) * HEAD]

        def rotated(index):
            return (head(index) * cosine + pltpu.roll(head(index), HEAD // 2, 1) * sine).astype(jnp.bfloat16)

        queries = jnp.concatenate([rotated(i) for i in range(QPG)], axis=0)
        return queries, rotated(QPG), head(QPG + 1).astype(jnp.bfloat16)

    def against(queries, keys):
        return lax.dot_general(queries, keys, (((1,), (1,)), ((), ())), preferred_element_type=jnp.float32)

    def attend(parts):
        highest = None
        for scores, _ in parts:
            top = jnp.max(scores, axis=1, keepdims=True)
            highest = top if highest is None else jnp.maximum(highest, top)
        total = None
        output = None
        for scores, values in parts:
            expo = jnp.exp2((scores - highest) * FACTOR)
            part_total = jnp.sum(expo, axis=1, keepdims=True)
            part_out = jnp.dot(expo.astype(jnp.bfloat16), values, preferred_element_type=jnp.float32)
            total = part_total if total is None else total + part_total
            output = part_out if output is None else output + part_out
        return (output / total).astype(jnp.bfloat16)

    def iota(shape, dim):
        return lax.broadcasted_iota(jnp.int32, shape, dim)

    def column_of(row):
        n = row.shape[1]
        square = jnp.where(iota((n, n), 0) == iota((n, n), 1), row.astype(jnp.float32), 0.0)
        return jnp.sum(square, axis=1, keepdims=True)

    def prepare():
        lengths = column_of(tail_len[...])
        block_pos = (iota((block_rows, 1), 0) + offset[0]).astype(jnp.float32)
        for start, rows, position in (
            (0, group_rows, prompt.shape[0] + lengths), (group_rows, block_rows, block_pos),
        ):
            angle = position * freq[...]
            cosines[pl.ds(start, rows), :] = jnp.cos(angle)
            sine = jnp.sin(angle)
            sines[pl.ds(start, rows), :] = jnp.where(iota(sine.shape, 1) < HEAD // 2, -sine, sine)

    def places():
        pages = table.shape[1]
        slots = pool.shape[0]
        page_column = column_of(table[...])
        matches = page_column == iota((pages, pages), 1).astype(jnp.float32)
        inverse = jnp.sum(jnp.where(matches, iota((pages, pages), 0).astype(jnp.float32), 0.0), axis=0, keepdims=True)
        spread_out = jnp.where(iota((pages, slots), 1) // PAGE == iota((pages, slots), 0), 1.0, 0.0)
        inverse = jnp.broadcast_to(inverse, (8, pages)).astype(jnp.bfloat16)
        row = jnp.dot(inverse, spread_out.astype(jnp.bfloat16), preferred_element_type=jnp.float32)
        place_of[...] = row * PAGE + (iota((8, slots), 1) % PAGE).astype(jnp.float32)

    def decode():
        queries, own_keys, own_values = project(0, group_rows)
        count = QPG * group_rows
        slots = pool.shape[0] // group_rows
        request = iota((count, 1), 0) % group_rows
        lengths = jnp.concatenate([column_of(tail_len[...])] * QPG, axis=0)
        first = (request * slots).astype(jnp.float32)
        place = place_of[0:1, :]
        tail_scores = against(queries, pool[:, :HEAD])
        tail_scores = jnp.where((place >= first) & (place < first + lengths), tail_scores, MASKED)
        own_scores = against(queries, own_keys)
        own_scores = jnp.where(iota((1, group_rows), 1) == request, own_scores, MASKED)
        output = attend((
            (against(queries, prompt[:, :HEAD]), prompt[:, HEAD:]),
            (tail_scores, pool[:, HEAD:]),
            (own_scores, own_values),
        ))
        for h in range(QPG):
            moved[0, :, h * HEAD : (h + 1) * HEAD] = output[h * group_rows : (h + 1) * group_rows]

    def hop_start(bit):
        return send(moved.at[bit], landed.at[bit], partner(bit))

    def hop_end(bit, copy):
        copy.wait_recv()
        take = (jnp.full((1, 1), mask[0], jnp.int32) >> bit) & 1
        moved[bit + 1, :, :] = jnp.where(take == 1, landed[bit], moved[bit])

    def block(index):
        start, rows = CHUNKS[index]
        first = start - group_rows
        queries, keys, values = project(start, rows)
        keys_new[pl.ds(first, rows), :] = keys
        values_new[pl.ds(first, rows), :] = values
        bias = jnp.where(iota((1, ctx.shape[0]), 1) < offset[0], 0.0, MASKED)
        parts = [(against(queries, ctx[:, :HEAD]) + bias, ctx[:, HEAD:])]
        seen = first + rows
        inside = against(queries, keys_new[pl.ds(0, seen), :])
        token = first + iota((QPG * rows, 1), 0) % rows
        inside = jnp.where(iota((1, seen), 1) <= token, inside, MASKED)
        parts.append((inside, values_new[pl.ds(0, seen), :]))
        output = attend(parts)
        for h in range(QPG):
            out_rows[pl.ds(first, rows), h * HEAD : (h + 1) * HEAD] = output[h * rows : (h + 1) * rows]
        view = pl.ds(first, rows)
        copy = pltpu.make_async_copy(out_rows.at[view], block_out.at[view], local_sem.at[6 + index])
        copy.start()
        return copy

    received = []
    copies_out = []
    prepare()
    places()
    received += forward_own(0)
    near = [None] * len(CHUNKS)
    far = [None] * len(CHUNKS)
    near[0] = spread(0)
    locals_[0].wait()
    locals_[1].wait()
    locals_[2].wait()
    for copy in received:
        copy.wait_recv()
    early_half(0, 32)
    far[0] = forward_far(0, near[0])
    fwd1 = forward_own(1)
    for copy in far[0]:
        copy.wait_recv()
    locals_[3].wait()
    locals_[4].wait()
    decode()
    locals_[5].wait()
    fwd2 = forward_own(2)
    hop = hop_start(0)
    for copy in fwd1:
        copy.wait_recv()
    early_half(32, 96)
    near[1] = spread(1)
    hop_end(0, hop)
    hop = hop_start(1)
    early_half(128, 96)
    far[1] = forward_far(1, near[1])
    for copy in far[1]:
        copy.wait_recv()
    hop_end(1, hop)
    hop = hop_start(2)
    copies_out.append(block(1))
    for copy in fwd2:
        copy.wait_recv()
    near[2] = spread(2)
    hop_end(2, hop)
    hop = hop_start(3)
    early_half(224, 96)
    far[2] = forward_far(2, near[2])
    for copy in far[2]:
        copy.wait_recv()
    hop_end(3, hop)
    hop = hop_start(4)
    copies_out.append(block(2))
    near[3] = spread(3)
    hop_end(4, hop)
    hop = hop_start(5)
    early_half(320, 96)
    far[3] = forward_far(3, near[3])
    for copy in far[3]:
        copy.wait_recv()
    hop_end(5, hop)
    copy = pltpu.make_async_copy(moved.at[HOPS], decode_out, local_sem.at[6])
    copy.start()
    copies_out.append(copy)
    copies_out.append(block(3))
    near[4] = spread(4)
    far[4] = forward_far(4, near[4])
    near[5] = spread(5)
    for copy in far[4]:
        copy.wait_recv()
    far[5] = forward_far(5, near[5])
    copies_out.append(block(4))
    for copy in far[5]:
        copy.wait_recv()
    copies_out.append(block(5))
    for copy in sent:
        copy.wait_send()
    for copy in copies_out:
        copy.wait()


def per_device(
    block_x, decode_x, gain, w_qkv, ctx_cache, prompt_cache, tail_pool, page_table, tail_len, block_offset, move_mask
):
    rows = block_x.shape[0] + decode_x.shape[0]
    depth = block_x.shape[1]
    frequency = np.power(THETA, -2.0 * np.arange(HEAD // 2) / HEAD).astype(np.float32)
    freq = jnp.asarray(np.concatenate([frequency, frequency])[None, :])
    hbm = pl.BlockSpec(memory_space=pl.ANY)
    vmem = pl.BlockSpec(memory_space=pltpu.VMEM)
    smem = pl.BlockSpec(memory_space=pltpu.SMEM)
    bf16, f32 = jnp.bfloat16, jnp.float32
    return pl.pallas_call(
        layer_kernel,
        out_shape=(
            jax.ShapeDtypeStruct(block_x.shape, bf16),
            jax.ShapeDtypeStruct(decode_x.shape, bf16),
        ),
        in_specs=[hbm, hbm, vmem, hbm, hbm, hbm, hbm, vmem, vmem, smem, smem, vmem],
        out_specs=(hbm, hbm),
        scratch_shapes=[
            pltpu.VMEM((8, rows, depth), bf16),
            pltpu.VMEM(w_qkv.shape, bf16),
            pltpu.VMEM(ctx_cache.shape, bf16),
            pltpu.VMEM(prompt_cache.shape, bf16),
            pltpu.VMEM(tail_pool.shape, bf16),
            pltpu.VMEM((8, tail_pool.shape[0]), f32),
            pltpu.VMEM((rows, w_qkv.shape[1]), f32),
            pltpu.VMEM((rows, 128), f32),
            pltpu.VMEM((rows, HEAD), f32),
            pltpu.VMEM((rows, HEAD), f32),
            pltpu.VMEM((block_x.shape[0], HEAD), bf16),
            pltpu.VMEM((block_x.shape[0], HEAD), bf16),
            pltpu.VMEM(block_x.shape, bf16),
            pltpu.VMEM((HOPS + 1,) + decode_x.shape, bf16),
            pltpu.VMEM((HOPS,) + decode_x.shape, bf16),
            pltpu.SemaphoreType.DMA((12,)),
            pltpu.SemaphoreType.DMA((64,)),
            pltpu.SemaphoreType.DMA((64,)),
        ],
        compiler_params=pltpu.CompilerParams(
            collective_id=0, has_side_effects=True, vmem_limit_bytes=56 * 2**20
        ),
        name="layer",
    )(
        block_x, decode_x, gain.astype(f32)[None, :], w_qkv, ctx_cache, prompt_cache, tail_pool,
        page_table, tail_len, block_offset, move_mask, freq,
    )


def solution(mesh):
    in_specs = (
        P("req", "tp"),
        P("req", "tp"),
        P(),
        P(None, "tp"),
        P("req", "tp"),
        P("req", "tp"),
        P("req", "tp"),
        P("req", None),
        P("req", None),
        P("req"),
        P(),
    )
    out_specs = (P("req", "tp"), P("req", "tp"))
    return jax.shard_map(
        per_device, mesh=mesh, in_specs=in_specs, out_specs=out_specs, check_vma=False
    )
```

time: 239 us -> 96.8 us (0.41)
  the two profiles are of different devices: /device:TPU:2 before, /device:TPU:64 now
where the time goes in v2:
time: 96.8 us; the launch traced here: 96.5 us
  Pallas kernels  90.1 us (93%)
  local copies, waits for them, and re-layouts  3.14 us (3%)
  between operations  1.93 us (2%)
  other arithmetic  1.3 us (1%)
    pallas_call x1, Pallas kernels, per_device(): pl.pallas_call(layer_kernel, out_shape=(jax.ShapeDtypeStruct(block_x.shap...  90.1 us
    unnamed x2, local copies, waits for them, and re-layouts  3.14 us

profile of v2, /device:TPU:64, one launch (start us, length us, event | category | flops | bytes accessed | tf_op | source)
XLA Modules:
  0.0 96.5 jit_solution(15258589720259097793)
XLA Ops:
  1.9 1.3 %broadcast_in_dim.7 = f32[4096]{0:T(1024)} convert(bf16[4096]{0:T(1024)(128)(2,1)} %param.14) | non-fusion elementwise | flops 4096 | bytes 24576 | tf_op jit(solution)/shard_map/broadcast_in_dim | solution.py:366
  3.2 90.1 %layer.1 = (bf16[384,512]{1,0:T(8,128)(2,1)}, bf16[32,512]{1,0:T(8,128)(2,1)}) custom-call(bf16[384,512]{1,0:T(8,128)(2,1)} %block_x.1, bf16[32,512]{1,0:T(8,128)(2,1)} %decode_x.1, f32[1,4096]{1,0:T(1,128)} %bitcast.1, bf16[4096,768]{1,0:T(8,128)(2,1)} %w_hbm.1, bf16[1024,256]{1,0:T(8,128)(2,1)} %ctx_hbm.1, bf16[512,256]{1,0:T(8,128)(2,1)} %prompt_hbm.1, ...), custom_call_target="tpu_custom_call" | custom-call | tf_op jit(solution)/shard_map/layer/pallas_call | solution.py:333
  93.3 1.8 %copy.18 = bf16[384,512]{1,0:T(8,128)(2,1)} copy(bf16[384,512]{1,0:T(8,128)(2,1)} %get-tuple-element.4) | data formatting | bytes 786432
  95.1 1.4 %copy.19 = bf16[32,512]{1,0:T(8,128)(2,1)} copy(bf16[32,512]{1,0:T(8,128)(2,1)} %get-tuple-element.5) | data formatting | bytes 65536

commit v3 on v2

--- a/solution.py
+++ b/solution.py
@@ -15,7 +15,7 @@
 THETA = 1000000.0
 PAGE = 16
 MESH = pl.DeviceIdType.MESH
-CHUNKS = ((0, 32), (32, 96), (128, 96), (224, 96), (320, 64), (384, 32))
+CHUNKS = ((0, 32), (32, 96), (128, 128), (256, 128), (384, 32))
 OWN = ((0, 32), (32, 192), (224, 192))
 HOPS = 6
 MASKED = -1e30
@@ -87,10 +87,10 @@
         [send(own_rows(s, n), gathered.at[tp, pl.ds(s, n)], along_y(d)) for d in directions] for s, n in OWN
     ]
 
-    def forward(arrived, start, rows, half):
+    def forward(near, start, rows, half):
         copies = []
         for which, d in enumerate(directions):
-            arrived[which].wait_recv()
+            near[which].wait_recv()
             slot = ((y - d + 4) % 4) * 2 + half
             view = gathered.at[slot, pl.ds(start + which * (rows // 2), rows // 2)]
             copies.append(send(view, view, along_y(d)))
@@ -105,8 +105,8 @@
         view = gathered.at[tp + 1 - 2 * zh, pl.ds(start, rows)]
         return [send(view, view, along_y(d)) for d in directions]
 
-    def forward_far(index, arrived):
-        return forward(arrived, CHUNKS[index][0], CHUNKS[index][1], 1 - zh)
+    def forward_far(index, near):
+        return forward(near, CHUNKS[index][0], CHUNKS[index][1], 1 - zh)
 
     def half_product(start, rows, half):
         total = None
@@ -115,7 +115,7 @@
             slot = 2 * j + half
             exact = gathered[slot, pl.ds(start, rows), :].astype(jnp.float32)
             base = pl.multiple_of(slot * depth, depth)
-            scaled = (exact * gain[:, pl.ds(base, depth)]).astype(jnp.bfloat16)
+            scaled = (exact * gain[pl.ds(base, depth)].astype(jnp.float32)[None, :]).astype(jnp.bfloat16)
             term = jnp.dot(scaled, w[pl.ds(base, depth), :], preferred_element_type=jnp.float32)
             total = term if total is None else total + term
             exact = exact * exact
@@ -242,81 +242,75 @@
         copy.start()
         return copy
 
-    received = []
     copies_out = []
+
+    def arrived(copies):
+        for copy in copies:
+            copy.wait_recv()
+
     prepare()
     places()
-    received += forward_own(0)
-    near = [None] * len(CHUNKS)
-    far = [None] * len(CHUNKS)
-    near[0] = spread(0)
-    locals_[0].wait()
-    locals_[1].wait()
-    locals_[2].wait()
-    for copy in received:
-        copy.wait_recv()
+    own0 = forward_own(0)
+    near0 = spread(0)
+    own1 = forward_own(1)
+    for copy in locals_[:3]:
+        copy.wait()
+    arrived(own0)
     early_half(0, 32)
-    far[0] = forward_far(0, near[0])
-    fwd1 = forward_own(1)
-    for copy in far[0]:
-        copy.wait_recv()
-    locals_[3].wait()
-    locals_[4].wait()
+    far0 = forward_far(0, near0)
+    own2 = forward_own(2)
+    arrived(own1)
+    early_half(32, 192)
+    for copy in locals_[3:]:
+        copy.wait()
+    arrived(far0)
     decode()
-    locals_[5].wait()
-    fwd2 = forward_own(2)
-    hop = hop_start(0)
-    for copy in fwd1:
-        copy.wait_recv()
-    early_half(32, 96)
-    near[1] = spread(1)
-    hop_end(0, hop)
-    hop = hop_start(1)
-    early_half(128, 96)
-    far[1] = forward_far(1, near[1])
-    for copy in far[1]:
-        copy.wait_recv()
-    hop_end(1, hop)
-    hop = hop_start(2)
-    copies_out.append(block(1))
-    for copy in fwd2:
-        copy.wait_recv()
+    hop = [hop_start(0)]
+
+    def hop_on():
+        bit = len(hop) - 1
+        if bit >= HOPS:
+            return
+        hop_end(bit, hop[bit])
+        if bit + 1 < HOPS:
+            hop.append(hop_start(bit + 1))
+            return
+        hop.append(pltpu.make_async_copy(moved.at[HOPS], decode_out, local_sem.at[6]))
+        hop[-1].start()
+        copies_out.append(hop[-1])
+
+    last = len(CHUNKS) - 1
+    near = {1: spread(1)}
+    hop_on()
+    arrived(own2)
+    early_half(224, 192)
     near[2] = spread(2)
-    hop_end(2, hop)
-    hop = hop_start(3)
-    early_half(224, 96)
-    far[2] = forward_far(2, near[2])
-    for copy in far[2]:
-        copy.wait_recv()
-    hop_end(3, hop)
-    hop = hop_start(4)
-    copies_out.append(block(2))
-    near[3] = spread(3)
-    hop_end(4, hop)
-    hop = hop_start(5)
-    early_half(320, 96)
-    far[3] = forward_far(3, near[3])
-    for copy in far[3]:
-        copy.wait_recv()
-    hop_end(5, hop)
-    copy = pltpu.make_async_copy(moved.at[HOPS], decode_out, local_sem.at[6])
-    copy.start()
-    copies_out.append(copy)
-    copies_out.append(block(3))
-    near[4] = spread(4)
-    far[4] = forward_far(4, near[4])
-    near[5] = spread(5)
-    for copy in far[4]:
-        copy.wait_recv()
-    far[5] = forward_far(5, near[5])
-    copies_out.append(block(4))
-    for copy in far[5]:
-        copy.wait_recv()
-    copies_out.append(block(5))
+    hop_on()
+    far = {1: forward_far(1, near[1])}
+    hop_on()
+    for k in range(3, last + 1):
+        near[k] = spread(k)
+        hop_on()
+        if k == last:
+            far[k - 1] = forward_far(k - 1, near[k - 1])
+        arrived(far[k - 2])
+        copies_out.append(block(k - 2))
+        if k < last:
+            far[k - 1] = forward_far(k - 1, near[k - 1])
+        hop_on()
+    far[last] = forward_far(last, near[last])
+    for k in (last - 1, last):
+        arrived(far[k])
+        copies_out.append(block(k))
     for copy in sent:
         copy.wait_send()
     for copy in copies_out:
         copy.wait()
+
+
+def finish_kernel(block_in, decode_in, block_out, decode_out):
+    block_out[...] = block_in[...]
+    decode_out[...] = decode_in[...]
 
 
 def per_device(
@@ -330,7 +324,7 @@
     vmem = pl.BlockSpec(memory_space=pltpu.VMEM)
     smem = pl.BlockSpec(memory_space=pltpu.SMEM)
     bf16, f32 = jnp.bfloat16, jnp.float32
-    return pl.pallas_call(
+    outputs = pl.pallas_call(
         layer_kernel,
         out_shape=(
             jax.ShapeDtypeStruct(block_x.shape, bf16),
@@ -363,9 +357,16 @@
         ),
         name="layer",
     )(
-        block_x, decode_x, gain.astype(f32)[None, :], w_qkv, ctx_cache, prompt_cache, tail_pool,
+        block_x, decode_x, gain, w_qkv, ctx_cache, prompt_cache, tail_pool,
         page_table, tail_len, block_offset, move_mask, freq,
     )
+    return pl.pallas_call(
+        finish_kernel,
+        out_shape=[jax.ShapeDtypeStruct(o.shape, o.dtype) for o in outputs],
+        in_specs=[vmem, vmem],
+        out_specs=[vmem, vmem],
+        name="finish",
+    )(*outputs)
 
 
 def solution(mesh):

time: 96.8 us -> 80.6 us (0.83)
  the two profiles are of different devices: /device:TPU:64 before, /device:TPU:2 now
where the time goes in v3:
time: 80.6 us; the launch traced here: 80.5 us
  Pallas kernels  78.5 us (97%)
  between operations  1.93 us (2%)
    pallas_call x1, Pallas kernels, per_device(): pl.pallas_call(layer_kernel, out_shape=(jax.ShapeDtypeStruct(block_x.shap...  76.7 us
    pallas_call x1, Pallas kernels, per_device(): pl.pallas_call(finish_kernel, out_shape=[jax.ShapeDtypeStruct(o.shape, o....  1.77 us

profile of v3, /device:TPU:2, one launch (start us, length us, event | category | flops | bytes accessed | tf_op | source)
XLA Modules:
  0.0 80.5 jit_solution(10534360913497198059)
XLA Ops:
  1.9 76.7 %layer.1 = (bf16[384,512]{1,0:T(8,128)(2,1)}, bf16[32,512]{1,0:T(8,128)(2,1)}) custom-call(bf16[384,512]{1,0:T(8,128)(2,1)} %block_x.1, bf16[32,512]{1,0:T(8,128)(2,1)} %decode_x.1, bf16[4096]{0:T(1024)(128)(2,1)} %gain.1, bf16[4096,768]{1,0:T(8,128)(2,1)} %w_hbm.1, bf16[1024,256]{1,0:T(8,128)(2,1)} %ctx_hbm.1, bf16[512,256]{1,0:T(8,128)(2,1)} %prompt_hbm.1, ...), custom_call_target="tpu_custom_call" | custom-call | tf_op jit(solution)/shard_map/layer/pallas_call | solution.py:327
  78.7 1.8 %finish.1 = (bf16[384,512]{1,0:T(8,128)(2,1)}, bf16[32,512]{1,0:T(8,128)(2,1)}) custom-call(bf16[384,512]{1,0:T(8,128)(2,1)} %get-tuple-element.4.block_in, bf16[32,512]{1,0:T(8,128)(2,1)} %get-tuple-element.5.decode_in), custom_call_target="tpu_custom_call" | custom-call | tf_op jit(solution)/shard_map/finish/pallas_call | solution.py:363

commit v4 on v3

--- a/solution.py
+++ b/solution.py
@@ -15,7 +15,7 @@
 THETA = 1000000.0
 PAGE = 16
 MESH = pl.DeviceIdType.MESH
-CHUNKS = ((0, 32), (32, 96), (128, 128), (256, 128), (384, 32))
+CHUNKS = ((0, 32), (32, 64), (96, 96), (192, 96), (288, 128))
 OWN = ((0, 32), (32, 192), (224, 192))
 HOPS = 6
 MASKED = -1e30

time: 80.6 us -> 78.4 us (0.973)
  the two profiles are of different devices: /device:TPU:2 before, /device:TPU:32 now
where the time goes in v4:
time: 78.4 us; the launch traced here: 78.2 us
  Pallas kernels  76.3 us (97%)
  between operations  1.93 us (2%)
    pallas_call x1, Pallas kernels, per_device(): pl.pallas_call(layer_kernel, out_shape=(jax.ShapeDtypeStruct(block_x.shap...  74.5 us
    pallas_call x1, Pallas kernels, per_device(): pl.pallas_call(finish_kernel, out_shape=[jax.ShapeDtypeStruct(o.shape, o....  1.77 us

profile of v4, /device:TPU:32, one launch (start us, length us, event | category | flops | bytes accessed | tf_op | source)
XLA Modules:
  0.0 78.2 jit_solution(9717033689049056085)
XLA Ops:
  1.9 74.5 %layer.1 = (bf16[384,512]{1,0:T(8,128)(2,1)}, bf16[32,512]{1,0:T(8,128)(2,1)}) custom-call(bf16[384,512]{1,0:T(8,128)(2,1)} %block_x.1, bf16[32,512]{1,0:T(8,128)(2,1)} %decode_x.1, bf16[4096]{0:T(1024)(128)(2,1)} %gain.1, bf16[4096,768]{1,0:T(8,128)(2,1)} %w_hbm.1, bf16[1024,256]{1,0:T(8,128)(2,1)} %ctx_hbm.1, bf16[512,256]{1,0:T(8,128)(2,1)} %prompt_hbm.1, ...), custom_call_target="tpu_custom_call" | custom-call | tf_op jit(solution)/shard_map/layer/pallas_call | solution.py:327
  76.4 1.8 %finish.1 = (bf16[384,512]{1,0:T(8,128)(2,1)}, bf16[32,512]{1,0:T(8,128)(2,1)}) custom-call(bf16[384,512]{1,0:T(8,128)(2,1)} %get-tuple-element.4.block_in, bf16[32,512]{1,0:T(8,128)(2,1)} %get-tuple-element.5.decode_in), custom_call_target="tpu_custom_call" | custom-call | tf_op jit(solution)/shard_map/finish/pallas_call | solution.py:363
